TPU v7x, 512 devices: a whole 4x8x8 slice. The times are simulated.
512 devices in a mesh: ctx: 64 (over y_hi, x, z), exp: 8 (over y_lo, core).
Axes of the slice: x: 4, y: 8 (y_hi: 2, y_lo: 4; y = y_hi * 4 + y_lo), z: 8, core: 2. Of those that a mesh axis runs over, the one named last changes fastest.
Arguments:
- queries: bfloat16 [4096, 6144], P('ctx', 'exp'), may hold values from -5 to 5
- keys: bfloat16 [4096, 1024], P('ctx', 'exp'), may hold values from -5 to 5
- values: bfloat16 [4096, 1024], P('ctx', 'exp'), may hold values from -16 to 16
- residual: bfloat16 [4096, 6144], P('ctx', 'exp'), may hold values from -25 to 25
- norm_gain: float32 [6144], P('exp'), may hold values from 0.5 to 1.5
- routes: int32 [4096, 1], P('ctx'), may hold values from 0 to 3; in each aligned block of 64 rows (0 to 63, 64 to 127, ...) at most 24 rows name the same one
- route_weight: float32 [4096], P('ctx'), may hold values from 0.25 to 1
- w_gate: bfloat16 [65536, 6144], P('ctx', 'exp'), may hold values from -0.078125 to 0.078125
- w_up: bfloat16 [65536, 6144], P('ctx', 'exp'), may hold values from -0.078125 to 0.078125
- w_down: bfloat16 [65536, 6144], P('ctx', 'exp'), may hold values from -0.046875 to 0.046875
Outputs:
- moe_out: bfloat16 [4096, 6144], P('ctx', 'exp')
Inputs may be any that keep to these rules, and one draw needn't show every extreme that they name: `routes`: within the 64 rows of one device, at most 24 tokens have the same route.
All inputs are finite; a program needn't handle non-finite values.
Results may differ from a plain program's by a relative error of at most 0.029.
Values may be sent and summed in bfloat16 or wider, within the bound.
No kernel may reach another device: no remote copies, remote signals or barrier semaphores. Data moves between devices by JAX's collectives and lax.ppermute only.
A program may use at most 64 MiB of HBM per device.

v0:
```python
import math
import jax
import jax.numpy as jnp
from jax import lax
from jax.sharding import Mesh, PartitionSpec as P

D = 6144
HD = 128
EXPERTS = 4
CAP = 24
CHUNKS = 2
F32 = jnp.float32
BF16 = jnp.bfloat16
CTX = ("yh", "xh", "xl", "z")
EXP = ("yl", "c")
HALF = ("xh", "xl", "z")
SWAP = [(0, 1), (1, 0)]
Y_XOR = [[(i, i ^ k) for i in range(4)] for k in range(4)]


def swap(x, axis):
    return lax.ppermute(x, axis, SWAP)


def split3(v):
    hi = lax.reduce_precision(v, 8, 7)
    mid = lax.reduce_precision(v - hi, 8, 7)
    lo = v - hi - mid
    return [p.astype(BF16) for p in (hi, mid, lo)]


def attend(queries, keys, values):
    rows = queries.shape[0]
    heads = queries.shape[1] // HD
    yh = lax.axis_index("yh")
    scale = 1.0 / math.sqrt(HD)
    foreign = lax.ppermute(queries, "yh", [(1, 0)])
    kv = jnp.concatenate([keys, values], axis=1)
    members = lax.axis_size(HALF)
    kv = lax.all_to_all(
        jnp.broadcast_to(kv[None], (members,) + kv.shape),
        HALF,
        split_axis=0,
        concat_axis=0,
        tiled=True,
    ).reshape(members * rows, 2 * HD)
    k_all, v_all = (kv[:, :HD], kv[:, HD:])
    count = members * rows

    def stacked(q):
        return q.reshape(rows, heads, HD).transpose(1, 0, 2).reshape(heads * rows, HD)

    q_all = jnp.concatenate([stacked(queries), stacked(foreign)], axis=0)
    own_pos = lax.axis_index(HALF) * rows + jnp.tile(jnp.arange(rows, dtype=jnp.int32), heads)
    limit = jnp.concatenate([own_pos, jnp.full_like(own_pos, count)])
    scores = jnp.einsum("qd,kd->qk", q_all, k_all, preferred_element_type=F32) * scale
    allowed = jnp.arange(count, dtype=jnp.int32)[None, :] <= limit[:, None]
    scores = jnp.where(allowed, scores, -1e30)
    top = jnp.max(scores, axis=1)
    weights = jnp.exp(scores - top[:, None])
    total = jnp.sum(weights, axis=1)
    acc = jnp.einsum("qk,kd->qd", weights.astype(BF16), v_all, preferred_element_type=F32)
    out = acc / total[:, None]
    lse = top + jnp.log(total)
    n = heads * rows

    def unstacked(o):
        return o.reshape(heads, rows, HD).transpose(1, 0, 2).reshape(rows, heads * HD)

    out_own, out_far = (unstacked(out[:n]), unstacked(out[n:]))
    lse_own, lse_far = (lse[:n].reshape(heads, rows).T, lse[n:].reshape(heads, rows).T)
    tail = jnp.concatenate(split3(lse_far), axis=1)
    tail = jnp.pad(tail, ((0, 0), (0, HD - tail.shape[1])))
    message = jnp.concatenate([out_far.astype(BF16), tail], axis=1)
    got = lax.ppermute(message, "yh", [(0, 1)])
    got_out = got[:, : heads * HD].astype(F32)
    parts = got[:, heads * HD : heads * HD + 3 * heads].astype(F32)
    got_lse = parts[:, :heads] + parts[:, heads : 2 * heads] + parts[:, 2 * heads :]
    share = jnp.where(yh == 1, jax.nn.sigmoid(got_lse - lse_own), 0.0)
    share = jnp.repeat(share, HD, axis=1)
    return (out_own * (1.0 - share) + got_out * share).astype(BF16)


def body(queries, keys, values, residual, norm_gain, routes, route_weight, w_gate, w_up, w_down):
    rows = queries.shape[0]
    feat = residual.shape[1]
    hidden_local = w_gate.shape[0]
    half = hidden_local // 2
    core = lax.axis_index("c")

    def halves(w, which):
        return lax.dynamic_slice_in_dim(w, which * half, half, axis=0)

    w_in = jnp.concatenate([halves(w_gate, core), halves(w_up, core)], axis=0)
    w_in_other = swap(
        jnp.concatenate([halves(w_gate, 1 - core), halves(w_up, 1 - core)], axis=0), "c"
    )
    w_out = halves(w_down, core)
    w_out_other = halves(w_down, 1 - core)
    attn = attend(queries, keys, values)
    mixed = residual.astype(F32) + attn.astype(F32)
    total_squares = lax.psum(jnp.sum(mixed * mixed, axis=1), EXP)
    normed = (mixed * lax.rsqrt(total_squares / D + 1e-05)[:, None] * norm_gain[None, :]).astype(
        BF16
    )
    chosen = routes[:, 0]
    expert_ids = jnp.arange(EXPERTS, dtype=jnp.int32)
    onehot = (chosen[:, None] == expert_ids[None, :]).astype(jnp.int32)
    slot_index = jnp.sum((jnp.cumsum(onehot, axis=0) - 1) * onehot, axis=1)
    slot_ids = jnp.arange(CAP, dtype=jnp.int32)
    select = (
        (chosen[None, None, :] == expert_ids[:, None, None])
        & (slot_index[None, None, :] == slot_ids[None, :, None])
    ).astype(BF16)
    packed = jnp.einsum("ect,td->ecd", select, normed, preferred_element_type=F32).astype(BF16)
    incoming = lax.all_to_all(packed, ("yh", "xh"), split_axis=0, concat_axis=0, tiled=True)
    nz = lax.axis_size("z")
    ny = lax.axis_size("yl")
    slots = CAP // CHUNKS
    block = EXPERTS * slots
    outs = []
    for k in range(CHUNKS):
        part = incoming[:, k * slots : (k + 1) * slots].reshape(block, feat)
        near = lax.all_to_all(
            jnp.broadcast_to(part[None], (nz, block, feat)),
            "z",
            split_axis=0,
            concat_axis=0,
            tiled=True,
        ).reshape(nz * block, feat)
        x = jnp.concatenate([near, swap(near, "xl")], axis=0)
        x_other = swap(x, "c")
        gate_up = jnp.einsum("rd,fd->rf", x, w_in, preferred_element_type=F32) + jnp.einsum(
            "rd,fd->rf", x_other, w_in_other, preferred_element_type=F32
        )
        n_rows = gate_up.shape[0]
        share = n_rows // ny
        gate_up = gate_up.astype(BF16).reshape(ny, share, 2 * half)
        me = lax.axis_index("yl")

        def piece(i):
            return lax.dynamic_index_in_dim(gate_up, me ^ i, 0, keepdims=False)

        full = piece(0).astype(F32)
        for i in range(1, ny):
            full = full + lax.ppermute(piece(i), "yl", Y_XOR[i]).astype(F32)
        hidden = (jax.nn.silu(full[:, :half]) * full[:, half:]).astype(BF16)
        hid = jnp.zeros((ny, share, half), BF16)
        hid = lax.dynamic_update_index_in_dim(hid, hidden, me, 0)
        for i in range(1, ny):
            hid = lax.dynamic_update_index_in_dim(
                hid, lax.ppermute(hidden, "yl", Y_XOR[i]), me ^ i, 0
            )
        hid = hid.reshape(n_rows, half)
        hid_other = swap(hid, "c")
        down = jnp.dot(hid, w_out, preferred_element_type=F32) + jnp.dot(
            hid_other, w_out_other, preferred_element_type=F32
        )
        stay, leave = (down[: n_rows // 2], down[n_rows // 2 :])
        summed = (stay + swap(leave.astype(BF16), "xl").astype(F32)).astype(BF16)
        back = lax.all_to_all(
            summed.reshape(nz, block, feat), "z", split_axis=0, concat_axis=0, tiled=True
        )
        outs.append(jnp.sum(back.astype(F32), axis=0).astype(BF16).reshape(EXPERTS, slots, feat))
    out = jnp.concatenate(outs, axis=1)
    returned = lax.all_to_all(out, ("yh", "xh"), split_axis=0, concat_axis=0, tiled=True)
    moe_rows = jnp.einsum("ect,ecd->td", select, returned, preferred_element_type=F32)
    return (route_weight[:, None] * moe_rows).astype(BF16)


def solution(mesh):
    fine = Mesh(mesh.devices.reshape(2, 2, 2, 8, 4, 2), CTX + EXP)
    wide = P(CTX, EXP)
    in_specs = (wide, wide, wide, wide, P(EXP), P(CTX, None), P(CTX), wide, wide, wide)
    return jax.shard_map(body, mesh=fine, in_specs=in_specs, out_specs=wide, check_vma=False)
```

profile of v0, /device:TPU:8, one launch (start us, length us, event | category | flops | bytes accessed | tf_op | source)
XLA Modules:
  0.0 368.0 jit_solution(5424616710159542530)
XLA Ops:
  2.0 13.2 %all-to-all-start = ((bf16[32,64,256]{2,1,0:T(8,128)(2,1)}), bf16[32,64,256]{2,1,0:T(8,128)(2,1)S(1)}, u32[]{:S(2)}, u32[]{:S(2)}) async-start(bf16[32,64,256]{2,1,0:T(8,128)(2,1)} %broadcast_in_dim.68), calls=%async_computation | async-start | bytes 2097152 | tf_op jit(solution)/shard_map/all_to_all | solution.py:40
  17.1 10.6 %collective-permute-done = bf16[64,768]{1,0:T(8,128)(2,1)S(1)} collective-permute-done((bf16[64,768]{1,0:T(8,128)(2,1)S(1)}, bf16[64,768]{1,0:T(8,128)(2,1)S(1)}, u32[]{:S(2)}, u32[]{:S(2)}) %collective-permute-start) | collective-permute-done | bytes 98336 | tf_op jit(solution)/shard_map/ppermute | solution.py:37
  27.8 15.9 %all-to-all-done = bf16[32,64,256]{2,1,0:T(8,128)(2,1)S(1)} async-done(((bf16[32,64,256]{2,1,0:T(8,128)(2,1)}), bf16[32,64,256]{2,1,0:T(8,128)(2,1)S(1)}, u32[]{:S(2)}, u32[]{:S(2)}) %all-to-all-start) | async-done | bytes 1048608 | tf_op jit(solution)/shard_map/all_to_all | solution.py:40
  45.1 2.1 fusion
  49.4 6.8 %collective-permute-start.1 = (bf16[64,896]{1,0:T(8,128)(2,1)S(1)}, bf16[64,896]{1,0:T(8,128)(2,1)S(1)}, u32[]{:S(2)}, u32[]{:S(2)}) collective-permute-start(bf16[64,896]{1,0:T(8,128)(2,1)S(1)} %fusion.34), channel_id=1, source_target_pairs={{0,256},{1,257},{2,258},{3,259},{4,260},{5,261},{6,262},{7,263},{8... | collective-permute-start | bytes 344072 | tf_op jit(solution)/shard_map/ppermute | solution.py:75
  56.6 3.2 collective-permute-done.1
  60.2 10.0 %psum.7 = f32[64]{0:T(128)S(1)} all-reduce(f32[64]{0:T(128)S(1)} %get-tuple-element.9), channel_id=1, replica_groups=mesh['yh'=2,'xh'=2,'xl'=2,'z'=8,'yl'=4,'c'=2] {'yl','c'}, use_global_device_ids=true, to_apply=%region_5.6 | all-reduce | flops 64 | bytes 512 | tf_op jit(solution)/shard_map/psum | solution.py:102
  70.5 20.1 %all_to_all.35 = bf16[4,24,768]{2,1,0:T(8,128)(2,1)S(1)} all-to-all(bf16[4,24,768]{2,1,0:T(8,128)(2,1)S(1)} %convolution_convert_fusion), channel_id=1, replica_groups=mesh['yh'=2,'xh'=2,'xl'=2,'z'=8,'yl'=4,'c'=2] {'yh','xh'}, dimensions={0} | all-to-all | bytes 294912 | tf_op jit(solution)/shard_map/all_to_all | solution.py:116
  91.5 4.8 %all-to-all-start.2 = ((bf16[8,48,768]{2,1,0:T(8,128)(2,1)}), bf16[8,48,768]{2,1,0:T(8,128)(2,1)S(1)}, u32[]{:S(2)}, u32[]{:S(2)}) async-start(bf16[8,48,768]{2,1,0:T(8,128)(2,1)} %broadcast_in_dim.73), calls=%async_computation.2 | async-start | bytes 1179648 | tf_op jit(solution)/shard_map/all_to_all | solution.py:124
  96.3 17.9 %all-to-all-done.2 = bf16[8,48,768]{2,1,0:T(8,128)(2,1)S(1)} async-done(((bf16[8,48,768]{2,1,0:T(8,128)(2,1)}), bf16[8,48,768]{2,1,0:T(8,128)(2,1)S(1)}, u32[]{:S(2)}, u32[]{:S(2)}) %all-to-all-start.2) | async-done | bytes 589856 | tf_op jit(solution)/shard_map/all_to_all | solution.py:124
  115.1 3.5 all-to-all-start.4
  118.6 1.9 collective-permute-start.2
  120.6 3.0 constant_dynamic-slice_fusion.2
  126.7 6.9 %collective-permute-done.2 = bf16[384,768]{1,0:T(8,128)(2,1)S(1)} collective-permute-done((bf16[384,768]{1,0:T(8,128)(2,1)S(1)}, bf16[384,768]{1,0:T(8,128)(2,1)S(1)}, u32[]{:S(2)}, u32[]{:S(2)}) %collective-permute-start.2) | collective-permute-done | bytes 589856 | tf_op jit(solution)/shard_map/ppermute | solution.py:22
  136.8 2.2 collective-permute-start.13
  139.0 15.4 %collective-permute-done.13 = bf16[384,768]{1,0:T(8,128)(2,1)S(1)} collective-permute-done((bf16[384,768]{1,0:T(8,128)(2,1)S(1)}, bf16[384,768]{1,0:T(8,128)(2,1)S(1)}, u32[]{:S(2)}, u32[]{:S(2)}) %collective-permute-start.13) | collective-permute-done | bytes 589856 | tf_op jit(solution)/shard_map/ppermute | solution.py:22
  158.4 3.3 fusion.67
  163.2 3.0 collective-permute-start.5
  166.2 3.4 collective-permute-start.6
  169.6 3.2 collective-permute-start.7
  172.8 3.2 fusion.68
  177.5 3.9 %collective-permute-start.15 = (bf16[192,1024]{1,0:T(8,128)(2,1)S(1)}, bf16[192,1024]{1,0:T(8,128)(2,1)S(1)}, u32[]{:S(2)}, u32[]{:S(2)}) collective-permute-start(bf16[192,1024]{1,0:T(8,128)(2,1)S(1)} %get-tuple-element.14), channel_id=1, source_target_pairs={{0,2},{2,0},{4,6},{6,4},{1,3},{3,1},{5,7},{7,5},{8,10},{10,8},{12,... | collective-permute-start | bytes 1179656 | tf_op jit(solution)/shard_map/ppermute | solution.py:146
  181.4 3.4 collective-permute-start.16
  184.8 2.5 collective-permute-start.17
  187.3 8.7 %collective-permute-done.6 = bf16[192,1024]{1,0:T(8,128)(2,1)S(1)} collective-permute-done((bf16[192,1024]{1,0:T(8,128)(2,1)S(1)}, bf16[192,1024]{1,0:T(8,128)(2,1)S(1)}, u32[]{:S(2)}, u32[]{:S(2)}) %collective-permute-start.6) | collective-permute-done | bytes 393248 | tf_op jit(solution)/shard_map/ppermute | solution.py:146
  196.0 26.7 %collective-permute-done.7 = bf16[192,1024]{1,0:T(8,128)(2,1)S(1)} collective-permute-done((bf16[192,1024]{1,0:T(8,128)(2,1)S(1)}, bf16[192,1024]{1,0:T(8,128)(2,1)S(1)}, u32[]{:S(2)}, u32[]{:S(2)}) %collective-permute-start.7) | collective-permute-done | bytes 393248 | tf_op jit(solution)/shard_map/ppermute | solution.py:146
  223.1 1.9 collective-permute-start.8
  225.1 4.4 %collective-permute-start.9 = (bf16[192,512]{1,0:T(8,128)(2,1)S(1)}, bf16[192,512]{1,0:T(8,128)(2,1)S(1)}, u32[]{:S(2)}, u32[]{:S(2)}) collective-permute-start(bf16[192,512]{1,0:T(8,128)(2,1)S(1)} %get-tuple-element.6), channel_id=1, source_target_pairs={{0,4},{2,6},{4,0},{6,2},{1,5},{3,7},{5,1},{7,3},{8,12},{10,14},{12... | collective-permute-start | bytes 589832 | tf_op jit(solution)/shard_map/ppermute | solution.py:152
  229.5 2.9 collective-permute-start.10
  232.4 15.6 %collective-permute-done.17 = bf16[192,1024]{1,0:T(8,128)(2,1)S(1)} collective-permute-done((bf16[192,1024]{1,0:T(8,128)(2,1)S(1)}, bf16[192,1024]{1,0:T(8,128)(2,1)S(1)}, u32[]{:S(2)}, u32[]{:S(2)}) %collective-permute-start.17) | collective-permute-done | bytes 393248 | tf_op jit(solution)/shard_map/ppermute | solution.py:146
  248.5 1.9 collective-permute-start.18
  250.8 4.9 %collective-permute-done.10 = bf16[192,512]{1,0:T(8,128)(2,1)S(1)} collective-permute-done((bf16[192,512]{1,0:T(8,128)(2,1)S(1)}, bf16[192,512]{1,0:T(8,128)(2,1)S(1)}, u32[]{:S(2)}, u32[]{:S(2)}) %collective-permute-start.10) | collective-permute-done | bytes 196640 | tf_op jit(solution)/shard_map/ppermute | solution.py:152
  255.7 1.9 collective-permute-start.11
  257.7 1.9 collective-permute-start.19
  259.6 3.3 collective-permute-start.20
  262.9 10.4 %collective-permute-done.19 = bf16[192,512]{1,0:T(8,128)(2,1)S(1)} collective-permute-done((bf16[192,512]{1,0:T(8,128)(2,1)S(1)}, bf16[192,512]{1,0:T(8,128)(2,1)S(1)}, u32[]{:S(2)}, u32[]{:S(2)}) %collective-permute-start.19) | collective-permute-done | bytes 196640 | tf_op jit(solution)/shard_map/ppermute | solution.py:152
  273.3 5.8 %collective-permute-done.20 = bf16[192,512]{1,0:T(8,128)(2,1)S(1)} collective-permute-done((bf16[192,512]{1,0:T(8,128)(2,1)S(1)}, bf16[192,512]{1,0:T(8,128)(2,1)S(1)}, u32[]{:S(2)}, u32[]{:S(2)}) %collective-permute-start.20) | collective-permute-done | bytes 196640 | tf_op jit(solution)/shard_map/ppermute | solution.py:152
  279.1 1.9 collective-permute-start.21
  282.7 2.2 collective-permute-start.12
  285.0 2.2 fusion.16
  287.2 13.2 %collective-permute-done.12 = bf16[384,768]{1,0:T(8,128)(2,1)S(1)} collective-permute-done((bf16[384,768]{1,0:T(8,128)(2,1)S(1)}, bf16[384,768]{1,0:T(8,128)(2,1)S(1)}, u32[]{:S(2)}, u32[]{:S(2)}) %collective-permute-start.12) | collective-permute-done | bytes 589856 | tf_op jit(solution)/shard_map/ppermute | solution.py:22
  301.3 6.8 %all-to-all-start.3 = ((bf16[8,48,768]{2,1,0:T(8,128)(2,1)}), bf16[8,48,768]{2,1,0:T(8,128)(2,1)S(1)}, u32[]{:S(2)}, u32[]{:S(2)}) async-start(bf16[8,48,768]{2,1,0:T(8,128)(2,1)} %bitcast.24), calls=%async_computation.3 | async-start | bytes 1179648 | tf_op jit(solution)/shard_map/all_to_all | solution.py:161
  308.2 2.4 convolution_add_fusion
  310.7 2.2 collective-permute-start.22
  312.9 14.4 %collective-permute-done.22 = bf16[384,768]{1,0:T(8,128)(2,1)S(1)} collective-permute-done((bf16[384,768]{1,0:T(8,128)(2,1)S(1)}, bf16[384,768]{1,0:T(8,128)(2,1)S(1)}, u32[]{:S(2)}, u32[]{:S(2)}) %collective-permute-start.22) | collective-permute-done | bytes 589856 | tf_op jit(solution)/shard_map/ppermute | solution.py:22
  328.2 6.9 %all-to-all-start.5 = ((bf16[8,48,768]{2,1,0:T(8,128)(2,1)}), bf16[8,48,768]{2,1,0:T(8,128)(2,1)S(1)}, u32[]{:S(2)}, u32[]{:S(2)}) async-start(bf16[8,48,768]{2,1,0:T(8,128)(2,1)} %bitcast.36), calls=%async_computation.5 | async-start | bytes 1179648 | tf_op jit(solution)/shard_map/all_to_all | solution.py:161
  335.3 17.2 %all-to-all-done.5 = bf16[8,48,768]{2,1,0:T(8,128)(2,1)S(1)} async-done(((bf16[8,48,768]{2,1,0:T(8,128)(2,1)}), bf16[8,48,768]{2,1,0:T(8,128)(2,1)S(1)}, u32[]{:S(2)}, u32[]{:S(2)}) %all-to-all-start.5) | async-done | bytes 589856 | tf_op jit(solution)/shard_map/all_to_all | solution.py:161
  352.6 14.5 %all_to_all.36 = bf16[4,24,768]{2,1,0:T(8,128)(2,1)S(1)} all-to-all(bf16[4,24,768]{2,1,0:T(8,128)(2,1)S(1)} %pad_maximum_fusion.6), channel_id=1, replica_groups=mesh['yh'=2,'xh'=2,'xl'=2,'z'=8,'yl'=4,'c'=2] {'yh','xh'}, dimensions={0} | all-to-all | bytes 294912 | tf_op jit(solution)/shard_map/all_to_all | solution.py:166
  (111 shorter events, 29.5 us)
Async XLA Ops:
  0.0 281.1 %copy-start = (bf16[1024,768]{1,0:T(8,128)(2,1)S(1)}, bf16[1024,768]{1,0:T(8,128)(2,1)}, u32[]{:S(2)}) copy-start(bf16[1024,768]{1,0:T(8,128)(2,1)} %param.19) | copy-start | bytes 4718596
  0.0 15.2 %copy-start.7 = (bf16[64,768]{1,0:T(8,128)(2,1)S(1)}, bf16[64,768]{1,0:T(8,128)(2,1)}, u32[]{:S(2)}) copy-start(bf16[64,768]{1,0:T(8,128)(2,1)} %param.10) | copy-start | bytes 294916
  0.0 16.6 %copy-start.9 = (s32[64,1]{0,1:T(1,128)S(1)}, s32[64,1]{0,1:T(1,128)}, u32[]{:S(2)}) copy-start(s32[64,1]{0,1:T(1,128)} %param.15) | copy-start | bytes 772
  2.0 41.8 %all-to-all-start = ((bf16[32,64,256]{2,1,0:T(8,128)(2,1)}), bf16[32,64,256]{2,1,0:T(8,128)(2,1)S(1)}, u32[]{:S(2)}, u32[]{:S(2)}) async-start(bf16[32,64,256]{2,1,0:T(8,128)(2,1)} %broadcast_in_dim.68), calls=%async_computation | async-start | bytes 2097152 | tf_op jit(solution)/shard_map/all_to_all | solution.py:40
  15.2 12.5 %collective-permute-start = (bf16[64,768]{1,0:T(8,128)(2,1)S(1)}, bf16[64,768]{1,0:T(8,128)(2,1)S(1)}, u32[]{:S(2)}, u32[]{:S(2)}) collective-permute-start(bf16[64,768]{1,0:T(8,128)(2,1)S(1)} %copy-done.7), channel_id=1, source_target_pairs={{256,0},{257,1},{258,2},{259,3},{260,4},{261,5},{262,6},{263,7},{2... | collective-permute-start | bytes 294920 | tf_op jit(solution)/shard_map/ppermute | solution.py:37
  49.0 11.0 %copy-start.6 = (bf16[64,768]{1,0:T(8,128)(2,1)S(1)}, bf16[64,768]{1,0:T(8,128)(2,1)}, u32[]{:S(2)}) copy-start(bf16[64,768]{1,0:T(8,128)(2,1)} %param.13) | copy-start | bytes 294916
  49.1 21.2 %copy-start.8 = (f32[768]{0:T(1024)S(1)}, f32[768]{0:T(1024)}, u32[]{:S(2)}) copy-start(f32[768]{0:T(1024)} %param.14) | copy-start | bytes 9220
  49.4 10.4 %collective-permute-start.1 = (bf16[64,896]{1,0:T(8,128)(2,1)S(1)}, bf16[64,896]{1,0:T(8,128)(2,1)S(1)}, u32[]{:S(2)}, u32[]{:S(2)}) collective-permute-start(bf16[64,896]{1,0:T(8,128)(2,1)S(1)} %fusion.34), channel_id=1, source_target_pairs={{0,256},{1,257},{2,258},{3,259},{4,260},{5,261},{6,262},{7,263},{8... | collective-permute-start | bytes 344072 | tf_op jit(solution)/shard_map/ppermute | solution.py:75
  91.5 22.7 %all-to-all-start.2 = ((bf16[8,48,768]{2,1,0:T(8,128)(2,1)}), bf16[8,48,768]{2,1,0:T(8,128)(2,1)S(1)}, u32[]{:S(2)}, u32[]{:S(2)}) async-start(bf16[8,48,768]{2,1,0:T(8,128)(2,1)} %broadcast_in_dim.73), calls=%async_computation.2 | async-start | bytes 1179648 | tf_op jit(solution)/shard_map/all_to_all | solution.py:124
  115.1 21.7 %all-to-all-start.4 = ((bf16[8,48,768]{2,1,0:T(8,128)(2,1)}), bf16[8,48,768]{2,1,0:T(8,128)(2,1)S(1)}, u32[]{:S(2)}, u32[]{:S(2)}) async-start(bf16[8,48,768]{2,1,0:T(8,128)(2,1)} %broadcast_in_dim.79), calls=%async_computation.4 | async-start | bytes 1179648 | tf_op jit(solution)/shard_map/all_to_all | solution.py:124
  118.6 15.0 %collective-permute-start.2 = (bf16[384,768]{1,0:T(8,128)(2,1)S(1)}, bf16[384,768]{1,0:T(8,128)(2,1)S(1)}, u32[]{:S(2)}, u32[]{:S(2)}) collective-permute-start(bf16[384,768]{1,0:T(8,128)(2,1)S(1)} %bitcast.107), channel_id=1, source_target_pairs={{0,64},{64,0},{1,65},{65,1},{2,66},{66,2},{3,67},{67,3},{4,68},{68... | collective-permute-start | bytes 1769480 | tf_op jit(solution)/shard_map/ppermute | solution.py:22
  124.8 33.6 %collective-permute-start.4 = (bf16[1024,768]{1,0:T(8,128)(2,1)}, bf16[1024,768]{1,0:T(8,128)(2,1)}, u32[]{:S(2)}, u32[]{:S(2)}) collective-permute-start(bf16[1024,768]{1,0:T(8,128)(2,1)} %pad_maximum_fusion.1), channel_id=1, source_target_pairs={{0,1},{1,0},{2,3},{3,2},{4,5},{5,4},{6,7},{7,6},{8,9},{9,8},{10,11... | collective-permute-start | bytes 4718600 | tf_op jit(solution)/shard_map/ppermute | solution.py:22
  133.7 1.2 copy-start.4
  134.9 23.5 %collective-permute-start.3 = (bf16[768,768]{1,0:T(8,128)(2,1)}, bf16[768,768]{1,0:T(8,128)(2,1)}, u32[]{:S(2)}, u32[]{:S(2)}) collective-permute-start(bf16[768,768]{1,0:T(8,128)(2,1)} %pad_maximum_fusion.2), channel_id=1, source_target_pairs={{0,1},{1,0},{2,3},{3,2},{4,5},{5,4},{6,7},{7,6},{8,9},{9,8},{10,11... | collective-permute-start | bytes 3538952 | tf_op jit(solution)/shard_map/ppermute | solution.py:22
  136.8 17.6 %collective-permute-start.13 = (bf16[384,768]{1,0:T(8,128)(2,1)S(1)}, bf16[384,768]{1,0:T(8,128)(2,1)S(1)}, u32[]{:S(2)}, u32[]{:S(2)}) collective-permute-start(bf16[384,768]{1,0:T(8,128)(2,1)S(1)} %bitcast.104), channel_id=1, source_target_pairs={{0,64},{64,0},{1,65},{65,1},{2,66},{66,2},{3,67},{67,3},{4,68},{68... | collective-permute-start | bytes 1769480 | tf_op jit(solution)/shard_map/ppermute | solution.py:22
  154.4 0.8 copy-start.2
  156.4 16.4 %collective-permute-start.14 = (bf16[768,768]{1,0:T(8,128)(2,1)}, bf16[768,768]{1,0:T(8,128)(2,1)}, u32[]{:S(2)}, u32[]{:S(2)}) collective-permute-start(bf16[768,768]{1,0:T(8,128)(2,1)} %pad_maximum_fusion.3), channel_id=1, source_target_pairs={{0,1},{1,0},{2,3},{3,2},{4,5},{5,4},{6,7},{7,6},{8,9},{9,8},{10,11... | collective-permute-start | bytes 3538952 | tf_op jit(solution)/shard_map/ppermute | solution.py:22
  158.4 3.3 copy-start.1
  158.4 3.3 copy-start.5
  163.2 21.6 %collective-permute-start.5 = (bf16[192,1024]{1,0:T(8,128)(2,1)S(1)}, bf16[192,1024]{1,0:T(8,128)(2,1)S(1)}, u32[]{:S(2)}, u32[]{:S(2)}) collective-permute-start(bf16[192,1024]{1,0:T(8,128)(2,1)S(1)} %get-tuple-element.11), channel_id=1, source_target_pairs={{0,2},{2,0},{4,6},{6,4},{1,3},{3,1},{5,7},{7,5},{8,10},{10,8},{12,... | collective-permute-start | bytes 1179656 | tf_op jit(solution)/shard_map/ppermute | solution.py:146
  166.2 29.7 %collective-permute-start.6 = (bf16[192,1024]{1,0:T(8,128)(2,1)S(1)}, bf16[192,1024]{1,0:T(8,128)(2,1)S(1)}, u32[]{:S(2)}, u32[]{:S(2)}) collective-permute-start(bf16[192,1024]{1,0:T(8,128)(2,1)S(1)} %get-tuple-element.13), channel_id=1, source_target_pairs={{0,4},{2,6},{4,0},{6,2},{1,5},{3,7},{5,1},{7,3},{8,12},{10,14},{12... | collective-permute-start | bytes 1179656 | tf_op jit(solution)/shard_map/ppermute | solution.py:146
  169.6 6.4 %copy-start.3 = (bf16[384,768]{1,0:T(8,128)(2,1)S(1)}, bf16[384,768]{1,0:T(8,128)(2,1)}, u32[]{:S(2)}) copy-start(bf16[384,768]{1,0:T(8,128)(2,1)} %copy-done.2) | copy-start | bytes 1769476
  169.6 53.1 %collective-permute-start.7 = (bf16[192,1024]{1,0:T(8,128)(2,1)S(1)}, bf16[192,1024]{1,0:T(8,128)(2,1)S(1)}, u32[]{:S(2)}, u32[]{:S(2)}) collective-permute-start(bf16[192,1024]{1,0:T(8,128)(2,1)S(1)} %get-tuple-element.12), channel_id=1, source_target_pairs={{0,6},{2,4},{4,2},{6,0},{1,7},{3,5},{5,3},{7,1},{8,14},{10,12},{12... | collective-permute-start | bytes 1179656 | tf_op jit(solution)/shard_map/ppermute | solution.py:146
  177.5 51.9 %collective-permute-start.15 = (bf16[192,1024]{1,0:T(8,128)(2,1)S(1)}, bf16[192,1024]{1,0:T(8,128)(2,1)S(1)}, u32[]{:S(2)}, u32[]{:S(2)}) collective-permute-start(bf16[192,1024]{1,0:T(8,128)(2,1)S(1)} %get-tuple-element.14), channel_id=1, source_target_pairs={{0,2},{2,0},{4,6},{6,4},{1,3},{3,1},{5,7},{7,5},{8,10},{10,8},{12,... | collective-permute-start | bytes 1179656 | tf_op jit(solution)/shard_map/ppermute | solution.py:146
  181.4 50.9 %collective-permute-start.16 = (bf16[192,1024]{1,0:T(8,128)(2,1)S(1)}, bf16[192,1024]{1,0:T(8,128)(2,1)S(1)}, u32[]{:S(2)}, u32[]{:S(2)}) collective-permute-start(bf16[192,1024]{1,0:T(8,128)(2,1)S(1)} %get-tuple-element.16), channel_id=1, source_target_pairs={{0,4},{2,6},{4,0},{6,2},{1,5},{3,7},{5,1},{7,3},{8,12},{10,14},{12... | collective-permute-start | bytes 1179656 | tf_op jit(solution)/shard_map/ppermute | solution.py:146
  184.8 63.2 %collective-permute-start.17 = (bf16[192,1024]{1,0:T(8,128)(2,1)S(1)}, bf16[192,1024]{1,0:T(8,128)(2,1)S(1)}, u32[]{:S(2)}, u32[]{:S(2)}) collective-permute-start(bf16[192,1024]{1,0:T(8,128)(2,1)S(1)} %get-tuple-element.15), channel_id=1, source_target_pairs={{0,6},{2,4},{4,2},{6,0},{1,7},{3,5},{5,3},{7,1},{8,14},{10,12},{12... | collective-permute-start | bytes 1179656 | tf_op jit(solution)/shard_map/ppermute | solution.py:146
  223.1 27.3 %collective-permute-start.8 = (bf16[192,512]{1,0:T(8,128)(2,1)S(1)}, bf16[192,512]{1,0:T(8,128)(2,1)S(1)}, u32[]{:S(2)}, u32[]{:S(2)}) collective-permute-start(bf16[192,512]{1,0:T(8,128)(2,1)S(1)} %get-tuple-element.6), channel_id=1, source_target_pairs={{0,2},{2,0},{4,6},{6,4},{1,3},{3,1},{5,7},{7,5},{8,10},{10,8},{12,... | collective-permute-start | bytes 589832 | tf_op jit(solution)/shard_map/ppermute | solution.py:152
  225.1 25.7 %collective-permute-start.9 = (bf16[192,512]{1,0:T(8,128)(2,1)S(1)}, bf16[192,512]{1,0:T(8,128)(2,1)S(1)}, u32[]{:S(2)}, u32[]{:S(2)}) collective-permute-start(bf16[192,512]{1,0:T(8,128)(2,1)S(1)} %get-tuple-element.6), channel_id=1, source_target_pairs={{0,4},{2,6},{4,0},{6,2},{1,5},{3,7},{5,1},{7,3},{8,12},{10,14},{12... | collective-permute-start | bytes 589832 | tf_op jit(solution)/shard_map/ppermute | solution.py:152
  229.5 26.2 %collective-permute-start.10 = (bf16[192,512]{1,0:T(8,128)(2,1)S(1)}, bf16[192,512]{1,0:T(8,128)(2,1)S(1)}, u32[]{:S(2)}, u32[]{:S(2)}) collective-permute-start(bf16[192,512]{1,0:T(8,128)(2,1)S(1)} %get-tuple-element.6), channel_id=1, source_target_pairs={{0,6},{2,4},{4,2},{6,0},{1,7},{3,5},{5,3},{7,1},{8,14},{10,12},{12... | collective-permute-start | bytes 589832 | tf_op jit(solution)/shard_map/ppermute | solution.py:152
  248.5 14.4 %collective-permute-start.18 = (bf16[192,512]{1,0:T(8,128)(2,1)S(1)}, bf16[192,512]{1,0:T(8,128)(2,1)S(1)}, u32[]{:S(2)}, u32[]{:S(2)}) collective-permute-start(bf16[192,512]{1,0:T(8,128)(2,1)S(1)} %get-tuple-element.8), channel_id=1, source_target_pairs={{0,2},{2,0},{4,6},{6,4},{1,3},{3,1},{5,7},{7,5},{8,10},{10,8},{12,... | collective-permute-start | bytes 589832 | tf_op jit(solution)/shard_map/ppermute | solution.py:152
  255.7 25.3 %collective-permute-start.11 = (bf16[768,512]{1,0:T(8,128)(2,1)S(1)}, bf16[768,512]{1,0:T(8,128)(2,1)S(1)}, u32[]{:S(2)}, u32[]{:S(2)}) collective-permute-start(bf16[768,512]{1,0:T(8,128)(2,1)S(1)} %bitcast.102), channel_id=1, source_target_pairs={{0,1},{1,0},{2,3},{3,2},{4,5},{5,4},{6,7},{7,6},{8,9},{9,8},{10,11... | collective-permute-start | bytes 2359304 | tf_op jit(solution)/shard_map/ppermute | solution.py:22
  257.7 15.6 %collective-permute-start.19 = (bf16[192,512]{1,0:T(8,128)(2,1)S(1)}, bf16[192,512]{1,0:T(8,128)(2,1)S(1)}, u32[]{:S(2)}, u32[]{:S(2)}) collective-permute-start(bf16[192,512]{1,0:T(8,128)(2,1)S(1)} %get-tuple-element.8), channel_id=1, source_target_pairs={{0,4},{2,6},{4,0},{6,2},{1,5},{3,7},{5,1},{7,3},{8,12},{10,14},{12... | collective-permute-start | bytes 589832 | tf_op jit(solution)/shard_map/ppermute | solution.py:152
  259.6 19.5 %collective-permute-start.20 = (bf16[192,512]{1,0:T(8,128)(2,1)S(1)}, bf16[192,512]{1,0:T(8,128)(2,1)S(1)}, u32[]{:S(2)}, u32[]{:S(2)}) collective-permute-start(bf16[192,512]{1,0:T(8,128)(2,1)S(1)} %get-tuple-element.8), channel_id=1, source_target_pairs={{0,6},{2,4},{4,2},{6,0},{1,7},{3,5},{5,3},{7,1},{8,14},{10,12},{12... | collective-permute-start | bytes 589832 | tf_op jit(solution)/shard_map/ppermute | solution.py:152
  279.1 5.8 %collective-permute-start.21 = (bf16[768,512]{1,0:T(8,128)(2,1)S(1)}, bf16[768,512]{1,0:T(8,128)(2,1)S(1)}, u32[]{:S(2)}, u32[]{:S(2)}) collective-permute-start(bf16[768,512]{1,0:T(8,128)(2,1)S(1)} %bitcast.100), channel_id=1, source_target_pairs={{0,1},{1,0},{2,3},{3,2},{4,5},{5,4},{6,7},{7,6},{8,9},{9,8},{10,11... | collective-permute-start | bytes 2359304 | tf_op jit(solution)/shard_map/ppermute | solution.py:22
  282.7 17.6 %collective-permute-start.12 = (bf16[384,768]{1,0:T(8,128)(2,1)S(1)}, bf16[384,768]{1,0:T(8,128)(2,1)S(1)}, u32[]{:S(2)}, u32[]{:S(2)}) collective-permute-start(bf16[384,768]{1,0:T(8,128)(2,1)S(1)} %slice.157), channel_id=1, source_target_pairs={{0,64},{64,0},{1,65},{65,1},{2,66},{66,2},{3,67},{67,3},{4,68},{68... | collective-permute-start | bytes 1769480 | tf_op jit(solution)/shard_map/ppermute | solution.py:22
  301.3 26.9 %all-to-all-start.3 = ((bf16[8,48,768]{2,1,0:T(8,128)(2,1)}), bf16[8,48,768]{2,1,0:T(8,128)(2,1)S(1)}, u32[]{:S(2)}, u32[]{:S(2)}) async-start(bf16[8,48,768]{2,1,0:T(8,128)(2,1)} %bitcast.24), calls=%async_computation.3 | async-start | bytes 1179648 | tf_op jit(solution)/shard_map/all_to_all | solution.py:161
  310.7 56.4 %copy-start.10 = (f32[64]{0:T(128)S(1)}, f32[64]{0:T(128)}, u32[]{:S(2)}) copy-start(f32[64]{0:T(128)} %param.16) | copy-start | bytes 772
  310.7 16.6 %collective-permute-start.22 = (bf16[384,768]{1,0:T(8,128)(2,1)S(1)}, bf16[384,768]{1,0:T(8,128)(2,1)S(1)}, u32[]{:S(2)}, u32[]{:S(2)}) collective-permute-start(bf16[384,768]{1,0:T(8,128)(2,1)S(1)} %slice.156), channel_id=1, source_target_pairs={{0,64},{64,0},{1,65},{65,1},{2,66},{66,2},{3,67},{67,3},{4,68},{68... | collective-permute-start | bytes 1769480 | tf_op jit(solution)/shard_map/ppermute | solution.py:22
  328.2 24.2 %all-to-all-start.5 = ((bf16[8,48,768]{2,1,0:T(8,128)(2,1)}), bf16[8,48,768]{2,1,0:T(8,128)(2,1)S(1)}, u32[]{:S(2)}, u32[]{:S(2)}) async-start(bf16[8,48,768]{2,1,0:T(8,128)(2,1)} %bitcast.36), calls=%async_computation.5 | async-start | bytes 1179648 | tf_op jit(solution)/shard_map/all_to_all | solution.py:161
where the time goes:
time: 369 us; the launch traced here: 368 us
  waiting for transfers between devices  187 us (51%)
  starting transfers between devices  97 us (26%)
  blocking collectives  44.6 us (12%)
  matrix products  19.7 us (5%)
  other arithmetic  10.2 us (3%)
  local copies, waits for them, and re-layouts  8.49 us (2%)
    ppermute x6, waiting for transfers between devices, body(): full = full + lax.ppermute(piece(i), 'yl', Y_XOR[i]).astype(F32)  51 us
    ppermute x9, waiting for transfers between devices, swap(): return lax.ppermute(x, axis, SWAP)  49.9 us
    ppermute x6, waiting for transfers between devices, body(): lax.ppermute(hidden, 'yl', Y_XOR[i])  21.5 us
    all_to_all x1, blocking collectives, body(): lax.all_to_all(packed, ('yh', 'xh'), split_axis=0, concat_axis=0, tiled=T...  20.1 us
    ppermute x6, starting transfers between devices, body(): full = full + lax.ppermute(piece(i), 'yl', Y_XOR[i]).astype(F32)  19.3 us
    ppermute x9, starting transfers between devices, swap(): return lax.ppermute(x, axis, SWAP)  18.1 us
    all_to_all x2, waiting for transfers between devices, body(): lax.all_to_all(jnp.broadcast_to(part[None], (nz, block, feat)), 'z', spli...  17.9 us
    all_to_all x2, waiting for transfers between devices, body(): lax.all_to_all(summed.reshape(nz, block, feat), 'z', split_axis=0, concat...  17.2 us
  transfers between devices with their start and end apart: 28, of which 16 were waited for; matrix products, arithmetic and copies ran while one was open for 7% of the time, Pallas kernels for 0%

commit v1 on v0

--- a/solution.py
+++ b/solution.py
@@ -99,7 +99,8 @@
     w_out_other = halves(w_down, 1 - core)
     attn = attend(queries, keys, values)
     mixed = residual.astype(F32) + attn.astype(F32)
-    total_squares = lax.psum(jnp.sum(mixed * mixed, axis=1), EXP)
+    field = jnp.sum(mixed * mixed, axis=1)
+    total_squares = lax.psum(lax.psum(field, "c"), "yl")
     normed = (mixed * lax.rsqrt(total_squares / D + 1e-05)[:, None] * norm_gain[None, :]).astype(
         BF16
     )

time: 369 us -> 364 us (0.986)
  waiting for transfers between devices: 187 us -> 181 us
    ppermute x9, waiting for transfers between devices: 49.9 us -> 46.2 us  [swap(): return lax.ppermute(x, axis, SWAP)]
    psum x1 -> x2, blocking collectives: 10 us -> 10.9 us  [body(): total_squares = lax.psum(lax.psum(field, 'c'), 'yl')]
  transfers between devices with their start and end apart: 28 -> 28, of which waited for: 16 -> 15; matrix products, arithmetic and copies ran while one was open for 7% -> 7% of each run, Pallas kernels for 0% -> 0%
where the time goes in v1:
time: 364 us; the launch traced here: 363 us
  waiting for transfers between devices  181 us (50%)
  starting transfers between devices  97.7 us (27%)
  blocking collectives  44.5 us (12%)
  matrix products  19.7 us (5%)
  other arithmetic  10.2 us (3%)
  local copies, waits for them, and re-layouts  8.61 us (2%)
    ppermute x6, waiting for transfers between devices, body(): full = full + lax.ppermute(piece(i), 'yl', Y_XOR[i]).astype(F32)  51 us
    ppermute x9, waiting for transfers between devices, swap(): return lax.ppermute(x, axis, SWAP)  46.2 us
    ppermute x6, waiting for transfers between devices, body(): lax.ppermute(hidden, 'yl', Y_XOR[i])  21.5 us
    ppermute x9, starting transfers between devices, swap(): return lax.ppermute(x, axis, SWAP)  19.6 us
    all_to_all x1, blocking collectives, body(): lax.all_to_all(packed, ('yh', 'xh'), split_axis=0, concat_axis=0, tiled=T...  19.2 us
    ppermute x6, starting transfers between devices, body(): full = full + lax.ppermute(piece(i), 'yl', Y_XOR[i]).astype(F32)  19.2 us
    all_to_all x2, waiting for transfers between devices, body(): lax.all_to_all(summed.reshape(nz, block, feat), 'z', split_axis=0, concat...  17.2 us
    all_to_all x1, waiting for transfers between devices, attend(): lax.all_to_all(jnp.broadcast_to(kv[None], (members,) + kv.shape), HALF, s...  15.9 us
  transfers between devices with their start and end apart: 28, of which 15 were waited for; matrix products, arithmetic and copies ran while one was open for 7% of the time, Pallas kernels for 0%

profile of v1, /device:TPU:8, one launch (start us, length us, event | category | flops | bytes accessed | tf_op | source)
XLA Modules:
  0.0 362.9 jit_solution(7593553249262115242)
XLA Ops:
  2.0 13.2 %all-to-all-start = ((bf16[32,64,256]{2,1,0:T(8,128)(2,1)}), bf16[32,64,256]{2,1,0:T(8,128)(2,1)S(1)}, u32[]{:S(2)}, u32[]{:S(2)}) async-start(bf16[32,64,256]{2,1,0:T(8,128)(2,1)} %broadcast_in_dim.68), calls=%async_computation | async-start | bytes 2097152 | tf_op jit(solution)/shard_map/all_to_all | solution.py:40
  17.1 10.6 %collective-permute-done = bf16[64,768]{1,0:T(8,128)(2,1)S(1)} collective-permute-done((bf16[64,768]{1,0:T(8,128)(2,1)S(1)}, bf16[64,768]{1,0:T(8,128)(2,1)S(1)}, u32[]{:S(2)}, u32[]{:S(2)}) %collective-permute-start) | collective-permute-done | bytes 98336 | tf_op jit(solution)/shard_map/ppermute | solution.py:37
  27.9 15.9 %all-to-all-done = bf16[32,64,256]{2,1,0:T(8,128)(2,1)S(1)} async-done(((bf16[32,64,256]{2,1,0:T(8,128)(2,1)}), bf16[32,64,256]{2,1,0:T(8,128)(2,1)S(1)}, u32[]{:S(2)}, u32[]{:S(2)}) %all-to-all-start) | async-done | bytes 1048608 | tf_op jit(solution)/shard_map/all_to_all | solution.py:40
  45.2 2.1 fusion
  49.5 6.8 %collective-permute-start.1 = (bf16[64,896]{1,0:T(8,128)(2,1)S(1)}, bf16[64,896]{1,0:T(8,128)(2,1)S(1)}, u32[]{:S(2)}, u32[]{:S(2)}) collective-permute-start(bf16[64,896]{1,0:T(8,128)(2,1)S(1)} %fusion.34), channel_id=1, source_target_pairs={{0,256},{1,257},{2,258},{3,259},{4,260},{5,261},{6,262},{7,263},{8... | collective-permute-start | bytes 344072 | tf_op jit(solution)/shard_map/ppermute | solution.py:75
  56.6 3.2 collective-permute-done.1
  60.3 2.5 psum.14
  62.7 8.5 %psum.15 = f32[64]{0:T(128)S(1)} all-reduce(f32[64]{0:T(128)S(1)} %psum.14), channel_id=1, replica_groups=mesh['yh'=2,'xh'=2,'xl'=2,'z'=8,'yl'=4,'c'=2] {'yl'}, use_global_device_ids=true, to_apply=%region_6.7 | all-reduce | flops 64 | bytes 512 | tf_op jit(solution)/shard_map/psum | solution.py:103
  71.4 19.2 %all_to_all.35 = bf16[4,24,768]{2,1,0:T(8,128)(2,1)S(1)} all-to-all(bf16[4,24,768]{2,1,0:T(8,128)(2,1)S(1)} %convolution_convert_fusion), channel_id=1, replica_groups=mesh['yh'=2,'xh'=2,'xl'=2,'z'=8,'yl'=4,'c'=2] {'yh','xh'}, dimensions={0} | all-to-all | bytes 294912 | tf_op jit(solution)/shard_map/all_to_all | solution.py:117
  91.6 4.9 %all-to-all-start.2 = ((bf16[8,48,768]{2,1,0:T(8,128)(2,1)}), bf16[8,48,768]{2,1,0:T(8,128)(2,1)S(1)}, u32[]{:S(2)}, u32[]{:S(2)}) async-start(bf16[8,48,768]{2,1,0:T(8,128)(2,1)} %broadcast_in_dim.73), calls=%async_computation.2 | async-start | bytes 1179648 | tf_op jit(solution)/shard_map/all_to_all | solution.py:125
  96.6 15.8 %all-to-all-done.2 = bf16[8,48,768]{2,1,0:T(8,128)(2,1)S(1)} async-done(((bf16[8,48,768]{2,1,0:T(8,128)(2,1)}), bf16[8,48,768]{2,1,0:T(8,128)(2,1)S(1)}, u32[]{:S(2)}, u32[]{:S(2)}) %all-to-all-start.2) | async-done | bytes 589856 | tf_op jit(solution)/shard_map/all_to_all | solution.py:125
  113.2 3.5 all-to-all-start.4
  116.8 2.5 collective-permute-start.2
  119.3 3.0 constant_dynamic-slice_fusion.2
  125.5 4.2 %collective-permute-done.2 = bf16[384,768]{1,0:T(8,128)(2,1)S(1)} collective-permute-done((bf16[384,768]{1,0:T(8,128)(2,1)S(1)}, bf16[384,768]{1,0:T(8,128)(2,1)S(1)}, u32[]{:S(2)}, u32[]{:S(2)}) %collective-permute-start.2) | collective-permute-done | bytes 589856 | tf_op jit(solution)/shard_map/ppermute | solution.py:22
  132.8 2.5 collective-permute-start.13
  135.3 15.1 %collective-permute-done.13 = bf16[384,768]{1,0:T(8,128)(2,1)S(1)} collective-permute-done((bf16[384,768]{1,0:T(8,128)(2,1)S(1)}, bf16[384,768]{1,0:T(8,128)(2,1)S(1)}, u32[]{:S(2)}, u32[]{:S(2)}) %collective-permute-start.13) | collective-permute-done | bytes 589856 | tf_op jit(solution)/shard_map/ppermute | solution.py:22
  154.4 3.3 fusion.67
  159.2 3.5 collective-permute-start.5
  162.7 1.9 collective-permute-start.6
  164.7 4.1 %collective-permute-start.7 = (bf16[192,1024]{1,0:T(8,128)(2,1)S(1)}, bf16[192,1024]{1,0:T(8,128)(2,1)S(1)}, u32[]{:S(2)}, u32[]{:S(2)}) collective-permute-start(bf16[192,1024]{1,0:T(8,128)(2,1)S(1)} %get-tuple-element.12), channel_id=1, source_target_pairs={{0,6},{2,4},{4,2},{6,0},{1,7},{3,5},{5,3},{7,1},{8,14},{10,12},{12... | collective-permute-start | bytes 1179656 | tf_op jit(solution)/shard_map/ppermute | solution.py:147
  168.8 3.2 fusion.68
  173.5 4.4 %collective-permute-start.15 = (bf16[192,1024]{1,0:T(8,128)(2,1)S(1)}, bf16[192,1024]{1,0:T(8,128)(2,1)S(1)}, u32[]{:S(2)}, u32[]{:S(2)}) collective-permute-start(bf16[192,1024]{1,0:T(8,128)(2,1)S(1)} %get-tuple-element.14), channel_id=1, source_target_pairs={{0,2},{2,0},{4,6},{6,4},{1,3},{3,1},{5,7},{7,5},{8,10},{10,8},{12,... | collective-permute-start | bytes 1179656 | tf_op jit(solution)/shard_map/ppermute | solution.py:147
  177.9 1.9 collective-permute-start.16
  179.9 3.4 collective-permute-start.17
  183.2 7.8 %collective-permute-done.6 = bf16[192,1024]{1,0:T(8,128)(2,1)S(1)} collective-permute-done((bf16[192,1024]{1,0:T(8,128)(2,1)S(1)}, bf16[192,1024]{1,0:T(8,128)(2,1)S(1)}, u32[]{:S(2)}, u32[]{:S(2)}) %collective-permute-start.6) | collective-permute-done | bytes 393248 | tf_op jit(solution)/shard_map/ppermute | solution.py:147
  191.0 27.6 %collective-permute-done.7 = bf16[192,1024]{1,0:T(8,128)(2,1)S(1)} collective-permute-done((bf16[192,1024]{1,0:T(8,128)(2,1)S(1)}, bf16[192,1024]{1,0:T(8,128)(2,1)S(1)}, u32[]{:S(2)}, u32[]{:S(2)}) %collective-permute-start.7) | collective-permute-done | bytes 393248 | tf_op jit(solution)/shard_map/ppermute | solution.py:147
  219.1 1.9 collective-permute-start.8
  221.0 3.5 collective-permute-start.9
  224.5 3.8 %collective-permute-start.10 = (bf16[192,512]{1,0:T(8,128)(2,1)S(1)}, bf16[192,512]{1,0:T(8,128)(2,1)S(1)}, u32[]{:S(2)}, u32[]{:S(2)}) collective-permute-start(bf16[192,512]{1,0:T(8,128)(2,1)S(1)} %get-tuple-element.6), channel_id=1, source_target_pairs={{0,6},{2,4},{4,2},{6,0},{1,7},{3,5},{5,3},{7,1},{8,14},{10,12},{12... | collective-permute-start | bytes 589832 | tf_op jit(solution)/shard_map/ppermute | solution.py:153
  228.4 15.6 %collective-permute-done.17 = bf16[192,1024]{1,0:T(8,128)(2,1)S(1)} collective-permute-done((bf16[192,1024]{1,0:T(8,128)(2,1)S(1)}, bf16[192,1024]{1,0:T(8,128)(2,1)S(1)}, u32[]{:S(2)}, u32[]{:S(2)}) %collective-permute-start.17) | collective-permute-done | bytes 393248 | tf_op jit(solution)/shard_map/ppermute | solution.py:147
  244.4 1.9 collective-permute-start.18
  246.4 5.3 %collective-permute-done.10 = bf16[192,512]{1,0:T(8,128)(2,1)S(1)} collective-permute-done((bf16[192,512]{1,0:T(8,128)(2,1)S(1)}, bf16[192,512]{1,0:T(8,128)(2,1)S(1)}, u32[]{:S(2)}, u32[]{:S(2)}) %collective-permute-start.10) | collective-permute-done | bytes 196640 | tf_op jit(solution)/shard_map/ppermute | solution.py:153
  251.7 1.9 collective-permute-start.11
  255.6 2.3 collective-permute-start.20
  258.0 11.3 %collective-permute-done.19 = bf16[192,512]{1,0:T(8,128)(2,1)S(1)} collective-permute-done((bf16[192,512]{1,0:T(8,128)(2,1)S(1)}, bf16[192,512]{1,0:T(8,128)(2,1)S(1)}, u32[]{:S(2)}, u32[]{:S(2)}) %collective-permute-start.19) | collective-permute-done | bytes 196640 | tf_op jit(solution)/shard_map/ppermute | solution.py:153
  269.3 4.9 %collective-permute-done.20 = bf16[192,512]{1,0:T(8,128)(2,1)S(1)} collective-permute-done((bf16[192,512]{1,0:T(8,128)(2,1)S(1)}, bf16[192,512]{1,0:T(8,128)(2,1)S(1)}, u32[]{:S(2)}, u32[]{:S(2)}) %collective-permute-start.20) | collective-permute-done | bytes 196640 | tf_op jit(solution)/shard_map/ppermute | solution.py:153
  274.2 1.9 collective-permute-start.21
  277.8 2.5 collective-permute-start.12
  280.3 2.2 fusion.16
  282.5 12.9 %collective-permute-done.12 = bf16[384,768]{1,0:T(8,128)(2,1)S(1)} collective-permute-done((bf16[384,768]{1,0:T(8,128)(2,1)S(1)}, bf16[384,768]{1,0:T(8,128)(2,1)S(1)}, u32[]{:S(2)}, u32[]{:S(2)}) %collective-permute-start.12) | collective-permute-done | bytes 589856 | tf_op jit(solution)/shard_map/ppermute | solution.py:22
  296.4 6.8 %all-to-all-start.3 = ((bf16[8,48,768]{2,1,0:T(8,128)(2,1)}), bf16[8,48,768]{2,1,0:T(8,128)(2,1)S(1)}, u32[]{:S(2)}, u32[]{:S(2)}) async-start(bf16[8,48,768]{2,1,0:T(8,128)(2,1)} %bitcast.24), calls=%async_computation.3 | async-start | bytes 1179648 | tf_op jit(solution)/shard_map/all_to_all | solution.py:162
  303.2 2.4 convolution_add_fusion
  305.7 2.5 collective-permute-start.22
  308.3 14.0 %collective-permute-done.22 = bf16[384,768]{1,0:T(8,128)(2,1)S(1)} collective-permute-done((bf16[384,768]{1,0:T(8,128)(2,1)S(1)}, bf16[384,768]{1,0:T(8,128)(2,1)S(1)}, u32[]{:S(2)}, u32[]{:S(2)}) %collective-permute-start.22) | collective-permute-done | bytes 589856 | tf_op jit(solution)/shard_map/ppermute | solution.py:22
  323.3 6.9 %all-to-all-start.5 = ((bf16[8,48,768]{2,1,0:T(8,128)(2,1)}), bf16[8,48,768]{2,1,0:T(8,128)(2,1)S(1)}, u32[]{:S(2)}, u32[]{:S(2)}) async-start(bf16[8,48,768]{2,1,0:T(8,128)(2,1)} %bitcast.36), calls=%async_computation.5 | async-start | bytes 1179648 | tf_op jit(solution)/shard_map/all_to_all | solution.py:162
  330.4 17.2 %all-to-all-done.5 = bf16[8,48,768]{2,1,0:T(8,128)(2,1)S(1)} async-done(((bf16[8,48,768]{2,1,0:T(8,128)(2,1)}), bf16[8,48,768]{2,1,0:T(8,128)(2,1)S(1)}, u32[]{:S(2)}, u32[]{:S(2)}) %all-to-all-start.5) | async-done | bytes 589856 | tf_op jit(solution)/shard_map/all_to_all | solution.py:162
  347.7 14.3 %all_to_all.36 = bf16[4,24,768]{2,1,0:T(8,128)(2,1)S(1)} all-to-all(bf16[4,24,768]{2,1,0:T(8,128)(2,1)S(1)} %pad_maximum_fusion.6), channel_id=1, replica_groups=mesh['yh'=2,'xh'=2,'xl'=2,'z'=8,'yl'=4,'c'=2] {'yh','xh'}, dimensions={0} | all-to-all | bytes 294912 | tf_op jit(solution)/shard_map/all_to_all | solution.py:167
  (112 shorter events, 31.2 us)
Async XLA Ops:
  0.0 276.1 %copy-start = (bf16[1024,768]{1,0:T(8,128)(2,1)S(1)}, bf16[1024,768]{1,0:T(8,128)(2,1)}, u32[]{:S(2)}) copy-start(bf16[1024,768]{1,0:T(8,128)(2,1)} %param.19) | copy-start | bytes 4718596
  0.0 15.2 %copy-start.7 = (bf16[64,768]{1,0:T(8,128)(2,1)S(1)}, bf16[64,768]{1,0:T(8,128)(2,1)}, u32[]{:S(2)}) copy-start(bf16[64,768]{1,0:T(8,128)(2,1)} %param.10) | copy-start | bytes 294916
  0.0 16.6 %copy-start.9 = (s32[64,1]{0,1:T(1,128)S(1)}, s32[64,1]{0,1:T(1,128)}, u32[]{:S(2)}) copy-start(s32[64,1]{0,1:T(1,128)} %param.15) | copy-start | bytes 772
  2.0 41.8 %all-to-all-start = ((bf16[32,64,256]{2,1,0:T(8,128)(2,1)}), bf16[32,64,256]{2,1,0:T(8,128)(2,1)S(1)}, u32[]{:S(2)}, u32[]{:S(2)}) async-start(bf16[32,64,256]{2,1,0:T(8,128)(2,1)} %broadcast_in_dim.68), calls=%async_computation | async-start | bytes 2097152 | tf_op jit(solution)/shard_map/all_to_all | solution.py:40
  15.2 12.5 %collective-permute-start = (bf16[64,768]{1,0:T(8,128)(2,1)S(1)}, bf16[64,768]{1,0:T(8,128)(2,1)S(1)}, u32[]{:S(2)}, u32[]{:S(2)}) collective-permute-start(bf16[64,768]{1,0:T(8,128)(2,1)S(1)} %copy-done.7), channel_id=1, source_target_pairs={{256,0},{257,1},{258,2},{259,3},{260,4},{261,5},{262,6},{263,7},{2... | collective-permute-start | bytes 294920 | tf_op jit(solution)/shard_map/ppermute | solution.py:37
  49.1 11.0 %copy-start.6 = (bf16[64,768]{1,0:T(8,128)(2,1)S(1)}, bf16[64,768]{1,0:T(8,128)(2,1)}, u32[]{:S(2)}) copy-start(bf16[64,768]{1,0:T(8,128)(2,1)} %param.13) | copy-start | bytes 294916
  49.1 22.1 %copy-start.8 = (f32[768]{0:T(1024)S(1)}, f32[768]{0:T(1024)}, u32[]{:S(2)}) copy-start(f32[768]{0:T(1024)} %param.14) | copy-start | bytes 9220
  49.5 10.4 %collective-permute-start.1 = (bf16[64,896]{1,0:T(8,128)(2,1)S(1)}, bf16[64,896]{1,0:T(8,128)(2,1)S(1)}, u32[]{:S(2)}, u32[]{:S(2)}) collective-permute-start(bf16[64,896]{1,0:T(8,128)(2,1)S(1)} %fusion.34), channel_id=1, source_target_pairs={{0,256},{1,257},{2,258},{3,259},{4,260},{5,261},{6,262},{7,263},{8... | collective-permute-start | bytes 344072 | tf_op jit(solution)/shard_map/ppermute | solution.py:75
  91.6 20.7 %all-to-all-start.2 = ((bf16[8,48,768]{2,1,0:T(8,128)(2,1)}), bf16[8,48,768]{2,1,0:T(8,128)(2,1)S(1)}, u32[]{:S(2)}, u32[]{:S(2)}) async-start(bf16[8,48,768]{2,1,0:T(8,128)(2,1)} %broadcast_in_dim.73), calls=%async_computation.2 | async-start | bytes 1179648 | tf_op jit(solution)/shard_map/all_to_all | solution.py:125
  113.2 19.5 %all-to-all-start.4 = ((bf16[8,48,768]{2,1,0:T(8,128)(2,1)}), bf16[8,48,768]{2,1,0:T(8,128)(2,1)S(1)}, u32[]{:S(2)}, u32[]{:S(2)}) async-start(bf16[8,48,768]{2,1,0:T(8,128)(2,1)} %broadcast_in_dim.79), calls=%async_computation.4 | async-start | bytes 1179648 | tf_op jit(solution)/shard_map/all_to_all | solution.py:125
  116.8 12.8 %collective-permute-start.2 = (bf16[384,768]{1,0:T(8,128)(2,1)S(1)}, bf16[384,768]{1,0:T(8,128)(2,1)S(1)}, u32[]{:S(2)}, u32[]{:S(2)}) collective-permute-start(bf16[384,768]{1,0:T(8,128)(2,1)S(1)} %bitcast.107), channel_id=1, source_target_pairs={{0,64},{64,0},{1,65},{65,1},{2,66},{66,2},{3,67},{67,3},{4,68},{68... | collective-permute-start | bytes 1769480 | tf_op jit(solution)/shard_map/ppermute | solution.py:22
  123.6 30.8 %collective-permute-start.4 = (bf16[1024,768]{1,0:T(8,128)(2,1)}, bf16[1024,768]{1,0:T(8,128)(2,1)}, u32[]{:S(2)}, u32[]{:S(2)}) collective-permute-start(bf16[1024,768]{1,0:T(8,128)(2,1)} %pad_maximum_fusion.1), channel_id=1, source_target_pairs={{0,1},{1,0},{2,3},{3,2},{4,5},{5,4},{6,7},{7,6},{8,9},{9,8},{10,11... | collective-permute-start | bytes 4718600 | tf_op jit(solution)/shard_map/ppermute | solution.py:22
  129.6 1.2 copy-start.4
  130.9 23.5 %collective-permute-start.3 = (bf16[768,768]{1,0:T(8,128)(2,1)}, bf16[768,768]{1,0:T(8,128)(2,1)}, u32[]{:S(2)}, u32[]{:S(2)}) collective-permute-start(bf16[768,768]{1,0:T(8,128)(2,1)} %pad_maximum_fusion.2), channel_id=1, source_target_pairs={{0,1},{1,0},{2,3},{3,2},{4,5},{5,4},{6,7},{7,6},{8,9},{9,8},{10,11... | collective-permute-start | bytes 3538952 | tf_op jit(solution)/shard_map/ppermute | solution.py:22
  132.8 17.6 %collective-permute-start.13 = (bf16[384,768]{1,0:T(8,128)(2,1)S(1)}, bf16[384,768]{1,0:T(8,128)(2,1)S(1)}, u32[]{:S(2)}, u32[]{:S(2)}) collective-permute-start(bf16[384,768]{1,0:T(8,128)(2,1)S(1)} %bitcast.104), channel_id=1, source_target_pairs={{0,64},{64,0},{1,65},{65,1},{2,66},{66,2},{3,67},{67,3},{4,68},{68... | collective-permute-start | bytes 1769480 | tf_op jit(solution)/shard_map/ppermute | solution.py:22
  150.4 0.8 copy-start.2
  152.4 16.4 %collective-permute-start.14 = (bf16[768,768]{1,0:T(8,128)(2,1)}, bf16[768,768]{1,0:T(8,128)(2,1)}, u32[]{:S(2)}, u32[]{:S(2)}) collective-permute-start(bf16[768,768]{1,0:T(8,128)(2,1)} %pad_maximum_fusion.3), channel_id=1, source_target_pairs={{0,1},{1,0},{2,3},{3,2},{4,5},{5,4},{6,7},{7,6},{8,9},{9,8},{10,11... | collective-permute-start | bytes 3538952 | tf_op jit(solution)/shard_map/ppermute | solution.py:22
  154.3 3.3 copy-start.1
  154.3 3.3 copy-start.5
  159.2 20.6 %collective-permute-start.5 = (bf16[192,1024]{1,0:T(8,128)(2,1)S(1)}, bf16[192,1024]{1,0:T(8,128)(2,1)S(1)}, u32[]{:S(2)}, u32[]{:S(2)}) collective-permute-start(bf16[192,1024]{1,0:T(8,128)(2,1)S(1)} %get-tuple-element.11), channel_id=1, source_target_pairs={{0,2},{2,0},{4,6},{6,4},{1,3},{3,1},{5,7},{7,5},{8,10},{10,8},{12,... | collective-permute-start | bytes 1179656 | tf_op jit(solution)/shard_map/ppermute | solution.py:147
  162.7 28.3 %collective-permute-start.6 = (bf16[192,1024]{1,0:T(8,128)(2,1)S(1)}, bf16[192,1024]{1,0:T(8,128)(2,1)S(1)}, u32[]{:S(2)}, u32[]{:S(2)}) collective-permute-start(bf16[192,1024]{1,0:T(8,128)(2,1)S(1)} %get-tuple-element.13), channel_id=1, source_target_pairs={{0,4},{2,6},{4,0},{6,2},{1,5},{3,7},{5,1},{7,3},{8,12},{10,14},{12... | collective-permute-start | bytes 1179656 | tf_op jit(solution)/shard_map/ppermute | solution.py:147
  164.7 7.3 %copy-start.3 = (bf16[384,768]{1,0:T(8,128)(2,1)S(1)}, bf16[384,768]{1,0:T(8,128)(2,1)}, u32[]{:S(2)}) copy-start(bf16[384,768]{1,0:T(8,128)(2,1)} %copy-done.2) | copy-start | bytes 1769476
  164.7 54.0 %collective-permute-start.7 = (bf16[192,1024]{1,0:T(8,128)(2,1)S(1)}, bf16[192,1024]{1,0:T(8,128)(2,1)S(1)}, u32[]{:S(2)}, u32[]{:S(2)}) collective-permute-start(bf16[192,1024]{1,0:T(8,128)(2,1)S(1)} %get-tuple-element.12), channel_id=1, source_target_pairs={{0,6},{2,4},{4,2},{6,0},{1,7},{3,5},{5,3},{7,1},{8,14},{10,12},{12... | collective-permute-start | bytes 1179656 | tf_op jit(solution)/shard_map/ppermute | solution.py:147
  173.5 51.0 %collective-permute-start.15 = (bf16[192,1024]{1,0:T(8,128)(2,1)S(1)}, bf16[192,1024]{1,0:T(8,128)(2,1)S(1)}, u32[]{:S(2)}, u32[]{:S(2)}) collective-permute-start(bf16[192,1024]{1,0:T(8,128)(2,1)S(1)} %get-tuple-element.14), channel_id=1, source_target_pairs={{0,2},{2,0},{4,6},{6,4},{1,3},{3,1},{5,7},{7,5},{8,10},{10,8},{12,... | collective-permute-start | bytes 1179656 | tf_op jit(solution)/shard_map/ppermute | solution.py:147
  177.9 50.4 %collective-permute-start.16 = (bf16[192,1024]{1,0:T(8,128)(2,1)S(1)}, bf16[192,1024]{1,0:T(8,128)(2,1)S(1)}, u32[]{:S(2)}, u32[]{:S(2)}) collective-permute-start(bf16[192,1024]{1,0:T(8,128)(2,1)S(1)} %get-tuple-element.16), channel_id=1, source_target_pairs={{0,4},{2,6},{4,0},{6,2},{1,5},{3,7},{5,1},{7,3},{8,12},{10,14},{12... | collective-permute-start | bytes 1179656 | tf_op jit(solution)/shard_map/ppermute | solution.py:147
  179.9 64.1 %collective-permute-start.17 = (bf16[192,1024]{1,0:T(8,128)(2,1)S(1)}, bf16[192,1024]{1,0:T(8,128)(2,1)S(1)}, u32[]{:S(2)}, u32[]{:S(2)}) collective-permute-start(bf16[192,1024]{1,0:T(8,128)(2,1)S(1)} %get-tuple-element.15), channel_id=1, source_target_pairs={{0,6},{2,4},{4,2},{6,0},{1,7},{3,5},{5,3},{7,1},{8,14},{10,12},{12... | collective-permute-start | bytes 1179656 | tf_op jit(solution)/shard_map/ppermute | solution.py:147
  219.1 27.3 %collective-permute-start.8 = (bf16[192,512]{1,0:T(8,128)(2,1)S(1)}, bf16[192,512]{1,0:T(8,128)(2,1)S(1)}, u32[]{:S(2)}, u32[]{:S(2)}) collective-permute-start(bf16[192,512]{1,0:T(8,128)(2,1)S(1)} %get-tuple-element.6), channel_id=1, source_target_pairs={{0,2},{2,0},{4,6},{6,4},{1,3},{3,1},{5,7},{7,5},{8,10},{10,8},{12,... | collective-permute-start | bytes 589832 | tf_op jit(solution)/shard_map/ppermute | solution.py:153
  221.0 25.4 %collective-permute-start.9 = (bf16[192,512]{1,0:T(8,128)(2,1)S(1)}, bf16[192,512]{1,0:T(8,128)(2,1)S(1)}, u32[]{:S(2)}, u32[]{:S(2)}) collective-permute-start(bf16[192,512]{1,0:T(8,128)(2,1)S(1)} %get-tuple-element.6), channel_id=1, source_target_pairs={{0,4},{2,6},{4,0},{6,2},{1,5},{3,7},{5,1},{7,3},{8,12},{10,14},{12... | collective-permute-start | bytes 589832 | tf_op jit(solution)/shard_map/ppermute | solution.py:153
  224.5 27.2 %collective-permute-start.10 = (bf16[192,512]{1,0:T(8,128)(2,1)S(1)}, bf16[192,512]{1,0:T(8,128)(2,1)S(1)}, u32[]{:S(2)}, u32[]{:S(2)}) collective-permute-start(bf16[192,512]{1,0:T(8,128)(2,1)S(1)} %get-tuple-element.6), channel_id=1, source_target_pairs={{0,6},{2,4},{4,2},{6,0},{1,7},{3,5},{5,3},{7,1},{8,14},{10,12},{12... | collective-permute-start | bytes 589832 | tf_op jit(solution)/shard_map/ppermute | solution.py:153
  244.4 13.5 %collective-permute-start.18 = (bf16[192,512]{1,0:T(8,128)(2,1)S(1)}, bf16[192,512]{1,0:T(8,128)(2,1)S(1)}, u32[]{:S(2)}, u32[]{:S(2)}) collective-permute-start(bf16[192,512]{1,0:T(8,128)(2,1)S(1)} %get-tuple-element.8), channel_id=1, source_target_pairs={{0,2},{2,0},{4,6},{6,4},{1,3},{3,1},{5,7},{7,5},{8,10},{10,8},{12,... | collective-permute-start | bytes 589832 | tf_op jit(solution)/shard_map/ppermute | solution.py:153
  251.7 24.4 %collective-permute-start.11 = (bf16[768,512]{1,0:T(8,128)(2,1)S(1)}, bf16[768,512]{1,0:T(8,128)(2,1)S(1)}, u32[]{:S(2)}, u32[]{:S(2)}) collective-permute-start(bf16[768,512]{1,0:T(8,128)(2,1)S(1)} %bitcast.102), channel_id=1, source_target_pairs={{0,1},{1,0},{2,3},{3,2},{4,5},{5,4},{6,7},{7,6},{8,9},{9,8},{10,11... | collective-permute-start | bytes 2359304 | tf_op jit(solution)/shard_map/ppermute | solution.py:22
  253.6 15.6 %collective-permute-start.19 = (bf16[192,512]{1,0:T(8,128)(2,1)S(1)}, bf16[192,512]{1,0:T(8,128)(2,1)S(1)}, u32[]{:S(2)}, u32[]{:S(2)}) collective-permute-start(bf16[192,512]{1,0:T(8,128)(2,1)S(1)} %get-tuple-element.8), channel_id=1, source_target_pairs={{0,4},{2,6},{4,0},{6,2},{1,5},{3,7},{5,1},{7,3},{8,12},{10,14},{12... | collective-permute-start | bytes 589832 | tf_op jit(solution)/shard_map/ppermute | solution.py:153
  255.6 18.6 %collective-permute-start.20 = (bf16[192,512]{1,0:T(8,128)(2,1)S(1)}, bf16[192,512]{1,0:T(8,128)(2,1)S(1)}, u32[]{:S(2)}, u32[]{:S(2)}) collective-permute-start(bf16[192,512]{1,0:T(8,128)(2,1)S(1)} %get-tuple-element.8), channel_id=1, source_target_pairs={{0,6},{2,4},{4,2},{6,0},{1,7},{3,5},{5,3},{7,1},{8,14},{10,12},{12... | collective-permute-start | bytes 589832 | tf_op jit(solution)/shard_map/ppermute | solution.py:153
  274.2 6.1 %collective-permute-start.21 = (bf16[768,512]{1,0:T(8,128)(2,1)S(1)}, bf16[768,512]{1,0:T(8,128)(2,1)S(1)}, u32[]{:S(2)}, u32[]{:S(2)}) collective-permute-start(bf16[768,512]{1,0:T(8,128)(2,1)S(1)} %bitcast.100), channel_id=1, source_target_pairs={{0,1},{1,0},{2,3},{3,2},{4,5},{5,4},{6,7},{7,6},{8,9},{9,8},{10,11... | collective-permute-start | bytes 2359304 | tf_op jit(solution)/shard_map/ppermute | solution.py:22
  277.8 17.6 %collective-permute-start.12 = (bf16[384,768]{1,0:T(8,128)(2,1)S(1)}, bf16[384,768]{1,0:T(8,128)(2,1)S(1)}, u32[]{:S(2)}, u32[]{:S(2)}) collective-permute-start(bf16[384,768]{1,0:T(8,128)(2,1)S(1)} %slice.157), channel_id=1, source_target_pairs={{0,64},{64,0},{1,65},{65,1},{2,66},{66,2},{3,67},{67,3},{4,68},{68... | collective-permute-start | bytes 1769480 | tf_op jit(solution)/shard_map/ppermute | solution.py:22
  296.4 26.9 %all-to-all-start.3 = ((bf16[8,48,768]{2,1,0:T(8,128)(2,1)}), bf16[8,48,768]{2,1,0:T(8,128)(2,1)S(1)}, u32[]{:S(2)}, u32[]{:S(2)}) async-start(bf16[8,48,768]{2,1,0:T(8,128)(2,1)} %bitcast.24), calls=%async_computation.3 | async-start | bytes 1179648 | tf_op jit(solution)/shard_map/all_to_all | solution.py:162
  305.7 56.3 %copy-start.10 = (f32[64]{0:T(128)S(1)}, f32[64]{0:T(128)}, u32[]{:S(2)}) copy-start(f32[64]{0:T(128)} %param.16) | copy-start | bytes 772
  305.7 16.6 %collective-permute-start.22 = (bf16[384,768]{1,0:T(8,128)(2,1)S(1)}, bf16[384,768]{1,0:T(8,128)(2,1)S(1)}, u32[]{:S(2)}, u32[]{:S(2)}) collective-permute-start(bf16[384,768]{1,0:T(8,128)(2,1)S(1)} %slice.156), channel_id=1, source_target_pairs={{0,64},{64,0},{1,65},{65,1},{2,66},{66,2},{3,67},{67,3},{4,68},{68... | collective-permute-start | bytes 1769480 | tf_op jit(solution)/shard_map/ppermute | solution.py:22
  323.3 24.2 %all-to-all-start.5 = ((bf16[8,48,768]{2,1,0:T(8,128)(2,1)}), bf16[8,48,768]{2,1,0:T(8,128)(2,1)S(1)}, u32[]{:S(2)}, u32[]{:S(2)}) async-start(bf16[8,48,768]{2,1,0:T(8,128)(2,1)} %bitcast.36), calls=%async_computation.5 | async-start | bytes 1179648 | tf_op jit(solution)/shard_map/all_to_all | solution.py:162
